TPU v7x, 32 devices: a whole 2x2x4 slice. The times are simulated.
32 devices in a mesh: dp: 4 (over x, core), fsdp: 8 (over z, y).
Axes of the slice: x: 2, y: 2, z: 4, core: 2. Of those that a mesh axis runs over, the one named last changes fastest.
Arguments:
- tokens: bfloat16 [64, 512, 768], P(('dp', 'fsdp')), may hold values from -6 to 6
- segment_ids: int32 [64, 512], P(('dp', 'fsdp')), may hold values from 0 to 32, as said below
- qkv_weight: bfloat16 [768, 576], P(('dp', 'fsdp')), may hold values from -0.4375 to 0.4375
- out_weight: bfloat16 [768, 768], P(('dp', 'fsdp')), may hold values from -2.5 to 2.5
- up_weight: bfloat16 [768, 768], P(('dp', 'fsdp')), may hold values from -0.4375 to 0.4375
- down_weight: bfloat16 [3072, 192], P(('dp', 'fsdp')), may hold values from -0.21875 to 0.21875
- biases: bfloat16 [6, 768], P(None, ('dp', 'fsdp')), may hold values from -1 to 1
- up_bias: bfloat16 [3072], P(('dp', 'fsdp')), may hold values from -2.5 to 2.5
- gains: bfloat16 [2, 768], P(None, ('dp', 'fsdp')), may hold values from 0.5 to 1.5
- cotangent: bfloat16 [64, 512, 768], P(('dp', 'fsdp')), may hold values from -6 to 6
Outputs:
- layer_out: bfloat16 [64, 512, 768], P(('dp', 'fsdp'))
- input_grad: float32 [64, 512, 768], P(('dp', 'fsdp'))
- qkv_grad: float32 [768, 576], P(('dp', 'fsdp'))
- out_grad: float32 [768, 768], P(('dp', 'fsdp'))
- up_grad: float32 [768, 768], P(('dp', 'fsdp'))
- down_grad: float32 [3072, 192], P(('dp', 'fsdp'))
- bias_grad: float32 [6, 768], P(None, ('dp', 'fsdp'))
- up_bias_grad: float32 [3072], P(('dp', 'fsdp'))
- gain_grad: float32 [2, 768], P(None, ('dp', 'fsdp'))
Inputs may be any that keep to these rules, and one draw needn't show every extreme that they name: `segment_ids`: in each row the real tokens carry document numbers from 1 upward that never fall, each document contiguous; after them come 0 to 64 padding tokens numbered 0, exactly 64 in the first row.
All inputs are finite; a program needn't handle non-finite values.
Results may differ from a plain program's by a relative error of at most 0.012.
The roundings to bfloat16 on the way count: a program that leaves them out, or rounds other values in their place, can miss the bound.
Values may be sent and summed in bfloat16 or wider, within the bound.
A program may use at most 128 MiB of HBM per device.

v0:
```python
from functools import partial
import jax
import jax.numpy as jnp
from jax import lax
from jax.sharding import PartitionSpec as P

HEADS = 12
GROUPS = 4
EPSILON = 1e-05
SCORE_SCALE = 0.125
NEG_FILL = -1e30


def group_apply(values, weight):
    parts = values.reshape(values.shape[0], GROUPS, -1)
    table = weight.reshape(GROUPS, parts.shape[2], -1)
    return jnp.einsum("ngc,gce->nge", parts, table, preferred_element_type=jnp.float32)


def normalize(hidden):
    centre = hidden - jnp.mean(hidden, -1, keepdims=True)
    spread = lax.rsqrt(jnp.mean(centre * centre, -1, keepdims=True) + EPSILON)
    return (centre * spread, spread)


def norm_back(upstream, gain, normed, spread):
    scaled = upstream * gain
    return spread * (
        scaled
        - jnp.mean(scaled, -1, keepdims=True)
        - normed * jnp.mean(scaled * normed, -1, keepdims=True)
    )


def block_scores(query_blk, keys_seq, seg_blk, seg_seq):
    raw = (
        jnp.einsum("qhd,khd->hqk", query_blk, keys_seq, preferred_element_type=jnp.float32)
        * SCORE_SCALE
    )
    allowed = (seg_seq != 0)[None, :] & (
        (seg_blk[:, None] == seg_seq[None, :]) | (seg_blk[:, None] == 0)
    )
    return jnp.where(allowed[None], raw, NEG_FILL)


def attend_forward(item):
    queries_s, keys_s, values_s, seg_s = item
    pieces, sums_log = ([], [])
    scores = block_scores(queries_s, keys_s, seg_s, seg_s)
    top = jnp.max(scores, -1, keepdims=True)
    expd = jnp.exp(scores - top)
    total = jnp.sum(expd, -1, keepdims=True)
    probs = (expd / total).astype(jnp.bfloat16)
    pieces.append(jnp.einsum("hqk,khd->qhd", probs, values_s, preferred_element_type=jnp.float32))
    sums_log.append((top + jnp.log(total))[..., 0])
    return (jnp.concatenate(pieces, 0), jnp.concatenate(sums_log, 1))


def attend_backward(item):
    queries_s, keys_s, values_s, seg_s, lse_s, grad_ctx_s = item
    length = queries_s.shape[0]
    block_rows = min(512, length)
    grad_keys = jnp.zeros(keys_s.shape, jnp.float32)
    grad_values = jnp.zeros(values_s.shape, jnp.float32)
    scores = block_scores(queries_s, keys_s, seg_s, seg_s)
    probs = jnp.exp(scores - lse_s[:, 0:block_rows, None])
    grad_values = grad_values + jnp.einsum(
        "hqk,qhd->khd", probs.astype(jnp.bfloat16), grad_ctx_s, preferred_element_type=jnp.float32
    )
    grad_probs = jnp.einsum(
        "qhd,khd->hqk", grad_ctx_s, values_s, preferred_element_type=jnp.float32
    )
    inner = jnp.sum(probs * grad_probs, -1, keepdims=True)
    grad_scores = (probs * (grad_probs - inner)).astype(jnp.bfloat16)
    query_parts = [
        jnp.einsum("hqk,khd->qhd", grad_scores, keys_s, preferred_element_type=jnp.float32)
        * SCORE_SCALE
    ]
    grad_keys = (
        grad_keys
        + jnp.einsum("hqk,qhd->khd", grad_scores, queries_s, preferred_element_type=jnp.float32)
        * SCORE_SCALE
    )
    return (jnp.concatenate(query_parts, 0), grad_keys, grad_values)


def reduce_ffn(up_grad, down_grad, up_bias_grad):
    return (
        lax.psum_scatter(up_grad, ("dp", "fsdp"), scatter_dimension=0, tiled=True),
        lax.psum_scatter(down_grad, ("dp", "fsdp"), scatter_dimension=0, tiled=True),
        lax.psum_scatter(up_bias_grad, ("dp", "fsdp"), scatter_dimension=0, tiled=True),
    )


def local(
    tokens,
    segment_ids,
    qkv_weight,
    out_weight,
    up_weight,
    down_weight,
    biases,
    up_bias,
    gains,
    cotangent,
):

    def fetch_attention():
        return (
            lax.all_gather(qkv_weight, ("dp", "fsdp"), axis=0, tiled=True),
            lax.all_gather(out_weight, ("dp", "fsdp"), axis=0, tiled=True),
            lax.all_gather(biases, ("dp", "fsdp"), axis=1, tiled=True),
            lax.all_gather(gains, ("dp", "fsdp"), axis=1, tiled=True),
        )

    def fetch_ffn():
        return (
            lax.all_gather(up_weight, ("dp", "fsdp"), axis=0, tiled=True),
            lax.all_gather(down_weight, ("dp", "fsdp"), axis=0, tiled=True),
            lax.all_gather(up_bias, ("dp", "fsdp"), axis=0, tiled=True),
        )

    qkv_full, out_full, bias_full, gain_full = fetch_attention()
    up_full, down_full, up_bias_full = fetch_ffn()
    count, length, width = tokens.shape
    rows = count * length
    group_w = width // GROUPS
    shape4 = (count, length, HEADS, width // HEADS)
    inputs = tokens.reshape(rows, width)
    bias_vals = bias_full.astype(jnp.float32)
    gain_vals = gain_full.astype(jnp.float32)
    mixed = group_apply(inputs, qkv_full)
    queries = (
        (mixed[:, :, :group_w].reshape(rows, width) + bias_vals[0])
        .astype(jnp.bfloat16)
        .reshape(shape4)
    )
    keys_all = (
        mixed[:, :, group_w : 2 * group_w].reshape(rows, width).astype(jnp.bfloat16).reshape(shape4)
    )
    values_all = (
        (mixed[:, :, 2 * group_w :].reshape(rows, width) + bias_vals[1])
        .astype(jnp.bfloat16)
        .reshape(shape4)
    )
    attended, lse = lax.map(attend_forward, (queries, keys_all, values_all, segment_ids))
    context = attended.reshape(rows, width).astype(jnp.bfloat16)
    hidden1 = (
        inputs.astype(jnp.float32)
        + jnp.dot(context, out_full, preferred_element_type=jnp.float32)
        + bias_vals[2]
    )
    normed1, spread1 = normalize(hidden1)
    layer1 = normed1 * gain_vals[0] + bias_vals[3]
    layer1_low = layer1.astype(jnp.bfloat16)
    pre_act = group_apply(layer1_low, up_full).reshape(rows, -1) + up_bias_full.astype(jnp.float32)
    activ, gelu_pull = jax.vjp(partial(jax.nn.gelu, approximate=False), pre_act)
    activ_low = activ.astype(jnp.bfloat16)
    hidden2 = layer1 + group_apply(activ_low, down_full).reshape(rows, width) + bias_vals[4]
    normed2, spread2 = normalize(hidden2)
    layer_out = (
        (normed2 * gain_vals[1] + bias_vals[5]).astype(jnp.bfloat16).reshape(count, length, width)
    )
    qkv_back, out_back, unused_bias, gain_back = fetch_attention()
    up_back, down_back, unused_up = fetch_ffn()
    gain_back = gain_back.astype(jnp.float32)
    grad_out = cotangent.reshape(rows, width).astype(jnp.float32)
    grad_h2 = norm_back(grad_out, gain_back[1], normed2, spread2)
    grad_f_low = grad_h2.astype(jnp.bfloat16).reshape(rows, GROUPS, group_w)
    down_grad = jnp.einsum(
        "lut,lux->utx",
        activ_low.reshape(rows, GROUPS, -1),
        grad_f_low,
        preferred_element_type=jnp.float32,
    ).reshape(-1, group_w)
    grad_act = jnp.einsum(
        "ipo,pso->ips",
        grad_f_low,
        down_back.reshape(GROUPS, -1, group_w),
        preferred_element_type=jnp.float32,
    ).reshape(rows, -1)
    grad_pre = gelu_pull(grad_act)[0].astype(jnp.bfloat16)
    up_bias_grad = jnp.sum(grad_pre, 0, dtype=jnp.float32)
    grad_pre_groups = grad_pre.reshape(rows, GROUPS, -1)
    up_grad = jnp.einsum(
        "ngc,ngf->gcf",
        layer1_low.reshape(rows, GROUPS, group_w),
        grad_pre_groups,
        preferred_element_type=jnp.float32,
    ).reshape(width, -1)
    grad_l1 = grad_h2 + jnp.einsum(
        "ngf,gcf->ngc",
        grad_pre_groups,
        up_back.reshape(GROUPS, group_w, -1),
        preferred_element_type=jnp.float32,
    ).reshape(rows, width)
    grad_h1 = norm_back(grad_l1, gain_back[0], normed1, spread1)
    grad_attn = grad_h1.astype(jnp.bfloat16)
    out_grad = jnp.einsum("nc,ne->ce", context, grad_attn, preferred_element_type=jnp.float32)
    grad_ctx = jnp.einsum(
        "ne,ce->nc", grad_attn, out_back, preferred_element_type=jnp.float32
    ).astype(jnp.bfloat16)
    grad_queries, grad_keys, grad_values = lax.map(
        attend_backward, (queries, keys_all, values_all, segment_ids, lse, grad_ctx.reshape(shape4))
    )
    grad_q = grad_queries.reshape(rows, width).astype(jnp.bfloat16)
    grad_k = grad_keys.reshape(rows, width).astype(jnp.bfloat16)
    grad_v = grad_values.reshape(rows, width).astype(jnp.bfloat16)
    grad_mixed = jnp.concatenate(
        [
            grad_q.reshape(rows, GROUPS, group_w),
            grad_k.reshape(rows, GROUPS, group_w),
            grad_v.reshape(rows, GROUPS, group_w),
        ],
        -1,
    )
    qkv_grad = jnp.einsum(
        "ngc,nge->gce",
        inputs.reshape(rows, GROUPS, group_w),
        grad_mixed,
        preferred_element_type=jnp.float32,
    ).reshape(width, -1)
    input_grad = grad_h1 + jnp.einsum(
        "nge,gce->ngc",
        grad_mixed,
        qkv_back.reshape(GROUPS, group_w, -1),
        preferred_element_type=jnp.float32,
    ).reshape(rows, width)
    bias_grad = jnp.stack(
        [
            jnp.sum(grad_q, 0, dtype=jnp.float32),
            jnp.sum(grad_v, 0, dtype=jnp.float32),
            jnp.sum(grad_h1, 0),
            jnp.sum(grad_l1, 0),
            jnp.sum(grad_h2, 0),
            jnp.sum(grad_out, 0),
        ]
    )
    gain_grad = jnp.stack([jnp.sum(grad_l1 * normed1, 0), jnp.sum(grad_out * normed2, 0)])
    qkv_sum, out_sum, bias_sum, gain_sum = (
        lax.psum_scatter(qkv_grad, ("dp", "fsdp"), scatter_dimension=0, tiled=True),
        lax.psum_scatter(out_grad, ("dp", "fsdp"), scatter_dimension=0, tiled=True),
        lax.psum_scatter(bias_grad, ("dp", "fsdp"), scatter_dimension=1, tiled=True),
        lax.psum_scatter(gain_grad, ("dp", "fsdp"), scatter_dimension=1, tiled=True),
    )
    ffn_sums = reduce_ffn(up_grad, down_grad, up_bias_grad)
    up_sum, down_sum, up_bias_sum = ffn_sums
    return (
        layer_out,
        input_grad.reshape(count, length, width),
        qkv_sum,
        out_sum,
        up_sum,
        down_sum,
        bias_sum,
        up_bias_sum,
        gain_sum,
    )


def solution(mesh):
    in_specs = (
        P(("dp", "fsdp"), None, None),
        P(("dp", "fsdp"), None),
        P(("dp", "fsdp"), None),
        P(("dp", "fsdp"), None),
        P(("dp", "fsdp"), None),
        P(("dp", "fsdp"), None),
        P(None, ("dp", "fsdp")),
        P(("dp", "fsdp")),
        P(None, ("dp", "fsdp")),
        P(("dp", "fsdp"), None, None),
    )
    out_specs = (
        P(("dp", "fsdp"), None, None),
        P(("dp", "fsdp"), None, None),
        P(("dp", "fsdp"), None),
        P(("dp", "fsdp"), None),
        P(("dp", "fsdp"), None),
        P(("dp", "fsdp"), None),
        P(None, ("dp", "fsdp")),
        P(("dp", "fsdp")),
        P(None, ("dp", "fsdp")),
    )
    return jax.shard_map(local, mesh=mesh, in_specs=in_specs, out_specs=out_specs, check_vma=False)
```

profile of v0, /device:TPU:0, one launch (start us, length us, event | category | flops | bytes accessed | tf_op | source)
XLA Modules:
  0.0 926.9 jit_solution(14447026839796752932)
XLA Ops:
  9.5 4.9 copy.94
  16.0 81.7 %all_gather.26 = bf16[768,576]{1,0:T(8,128)(2,1)} all-gather(bf16[24,576]{1,0:T(8,128)(2,1)S(1)} %copy-done.27), channel_id=1, replica_groups=mesh['dp'=4,'fsdp'=8] {'dp','fsdp'}, dimensions={0}, use_global_device_ids=true | all-gather | bytes 912384 | tf_op jit(solution)/shard_map/all_gather | solution.py:110
  97.7 3.8 reshape_reshape.4
  101.5 3.2 convolution_bitcast_fusion
  106.0 3.4 fusion.77
  109.6 37.1 %all-reduce = bf16[3072]{0:T(1024)(128)(2,1)S(1)} all-reduce(bf16[3072]{0:T(1024)(128)(2,1)S(1)} %dynamic-update-slice), channel_id=1, replica_groups=mesh['dp'=4,'fsdp'=8] {'dp','fsdp'}, use_global_device_ids=true, to_apply=%add | all-reduce | flops 3072 | bytes 12288
  146.7 65.6 %all-gather.1 = bf16[32,24,2]{1,2,0:T(2,128)(2,1)S(1)} all-gather(bf16[1,24,2]{1,2,0:T(2,128)(2,1)S(1)} %bitcast.304), channel_id=1, replica_groups=mesh['dp'=4,'fsdp'=8] {'dp','fsdp'}, dimensions={0}, use_global_device_ids=true | all-gather | bytes 3168 | tf_op jit(solution)/shard_map/all_gather | solution.py:113
  212.6 2.7 convert_reduce_fusion.3
  216.0 63.9 %all-gather = bf16[32,24,6]{1,2,0:T(8,128)(2,1)S(1)} all-gather(bf16[1,24,6]{1,2,0:T(8,128)(2,1)S(1)} %bitcast.303), channel_id=1, replica_groups=mesh['dp'=4,'fsdp'=8] {'dp','fsdp'}, dimensions={0}, use_global_device_ids=true | all-gather | bytes 9504 | tf_op jit(solution)/shard_map/all_gather | solution.py:112
  280.9 3.1 copy.125
  286.3 5.7 reshape.348
  296.1 5.7 reshape.347
  301.8 5.0 fusion.66
  308.1 21.2 %while.26 = (s32[]{:T(128)}, bf16[2,512,12,64]{1,3,2,0:T(8,128)(2,1)}, f32[2,12,512]{2,1,0:T(8,128)S(1)}, bf16[2,512,12,64]{1,3,2,0:T(8,128)(2,1)}, s32[2,512]{1...) while((s32[]{:T(128)}, ...), condition=%wide.region_3.4_spmd, body=%wide.region_0.3_spmd.sunk | while | flops 843836416 | bytes 42963044 | solution.py:146
  313.1 5.5 bitcast_dynamic-update-slice_fusion.10
  323.6 5.5 bitcast_dynamic-update-slice_fusion.10
  329.3 3.0 copy.100
  333.9 4.3 fusion.78
  341.6 33.3 %fusion.52 = (bf16[1024,4,768]{2,0,1:T(8,128)(2,1)}, f32[1024,4,768]{2,0,1:T(8,128)}, f32[4,1024,768]{2,1,0:T(8,128)}) fusion(f32[4,768]{1,0:T(4,128)S(1)} %reshape.363, bf16[1024,4,192]{0,2,1:T(8,128)(2,1)} %bitcast.281, bf16[4,192,768]{2,1,0:T(8,128)(2,1)} %bitcast.294), kind=kOutput, calls=%fused_computation.77 | convolution fusion | flops 1415577600 | bytes 34222080 | tf_op jit(solution)/shard_map/ngc,gce->nge/dot_general | solution.py:17
  374.9 5.6 fusion.79
  384.8 3.1 fusion.72
  390.5 15.7 %convert_reduce_fusion = (f32[4,768]{1,0:T(4,128)}, bf16[1024,4,768]{2,0,1:T(8,128)(2,1)}) fusion(f32[1024,4,768]{2,0,1:T(8,128)} %get-tuple-element.275, bf16[1024,4,192]{0,2,1:T(8,128)(2,1)S(1)} %bitcast.285, bf16[4,768,192]{2,1,0:T(8,128)(2,1)S(1)} %bitcast.293, f32[4,1024,768]{2,1,0:T(8,128)} %get-tuple-element.285, f32[4,768]{1,0:T(4,128)S(1)} %reshape.363), kind=kOutput, calls=%fused_computation.78 | convolution fusion | flops 1261433856 | bytes 34234368 | tf_op jit(solution)/shard_map/ipo,pso->ips/dot_general | solution.py:176
  406.2 5.1 fusion.80
  422.2 3.9 reshape.356
  426.0 2.9 copy.109
  433.0 49.2 %while.27 = (s32[]{:T(128)}, bf16[2,512,12,64]{1,3,2,0:T(8,128)(2,1)}, bf16[2,512,12,64]{1,3,2,0:T(8,128)(2,1)}, bf16[2,512,12,64]{1,3,2,0:T(8,128)(2,1)}, bf16[...) while((s32[]{:T(128)}, ...), condition=%wide.region_14.15_spmd, body=%wide.region_12.14_spmd.sunk | while | flops 2062019584 | bytes 143596848 | solution.py:203
  435.4 3.9 bitcast_dynamic-update-slice_fusion.14
  439.3 6.9 multiply_reduce_fusion.10
  446.2 7.1 multiply_convert_fusion.2
  459.9 3.9 bitcast_dynamic-update-slice_fusion.14
  463.8 6.9 multiply_reduce_fusion.10
  470.7 7.1 multiply_convert_fusion.2
  482.1 3.0 copy.111
  486.6 4.3 copy.112
  490.9 3.8 convert_element_type.135
  494.7 2.8 copy.110
  497.5 3.8 convert_element_type.131
  504.4 3.2 fusion.81
  507.7 6.7 fusion.84
  515.8 5.7 fusion.82
  521.7 5.2 fusion.69
  527.0 2.9 copy.124
  532.1 3.9 fusion.83
  539.2 39.6 %all-reduce.5 = (f32[6,768]{1,0:T(8,128)S(1)}, f32[3072]{0:T(1024)S(1)}, f32[2,768]{1,0:T(2,128)S(1)}) all-reduce(f32[6,768]{1,0:T(8,128)S(1)} %stack.36, f32[3072]{0:T(1024)S(1)} %reduce_sum.188, f32[2,768]{1,0:T(2,128)S(1)} %pad_maximum_fusion), channel_id=6, replica_groups=mesh['dp'=4,'fsdp'=8] {'dp','fsdp'}, use_global_device_ids=true, to_apply=%region_25.26.clone | all-reduce | flops 9216 | bytes 73728
  580.7 24.0 %reduce-scatter.17.cloned.1.call-done = f32[24,576]{1,0:T(8,128)} async-done(((f32[768,576]{1,0:T(8,128)}), f32[24,576]{1,0:T(8,128)}) %reduce-scatter.17.cloned.1.call-update) | async-done | bytes 55312
  604.7 106.4 %reduce-scatter.15.cloned.1.call-done = f32[96,192]{1,0:T(8,128)} async-done(((f32[3072,192]{1,0:T(8,128)}), f32[96,192]{1,0:T(8,128)}) %reduce-scatter.15.cloned.1.call-update) | async-done | bytes 73744
  711.1 103.7 %reduce-scatter.13.cloned.1.call-done = f32[24,768]{1,0:T(8,128)} async-done(((f32[768,768]{1,0:T(8,128)}), f32[24,768]{1,0:T(8,128)}) %reduce-scatter.13.cloned.1.call-update) | async-done | bytes 73744 | tf_op jit(solution)/shard_map/reduce_scatter | solution.py:89
  814.8 104.8 %reduce-scatter.11.cloned.1.call-done = f32[24,768]{1,0:T(8,128)} async-done(((f32[768,768]{1,0:T(8,128)}), f32[24,768]{1,0:T(8,128)}) %reduce-scatter.11.cloned.1.call-update) | async-done | bytes 73744 | tf_op jit(solution)/shard_map/reduce_scatter | solution.py:242
  (204 shorter events, 77.8 us)
Async XLA Ops:
  7.2 326.7 %all-gather.6.cloned.1.call-start = ((), (), s32[]{:S(2)}) async-start(), calls=%async_computation.4 | async-start | bytes 1216512 | tf_op jit(solution)/shard_map/all_gather | solution.py:111
  7.9 333.6 %all-gather.8.cloned.1.call-start = ((), (), s32[]{:S(2)}) async-start(), calls=%async_computation.5 | async-start | bytes 1216512 | tf_op jit(solution)/shard_map/all_gather | solution.py:118
  8.7 366.2 %all-gather.10.cloned.1.call-start = ((), (), s32[]{:S(2)}) async-start(), calls=%async_computation.6 | async-start | bytes 1622016 | tf_op jit(solution)/shard_map/all_gather | solution.py:119
  9.4 595.3 %reduce-scatter.17.cloned.1.call-start = ((), (), s32[]{:S(2)}) async-start(), calls=%async_computation.10 | async-start | bytes 2027520
  14.4 1.7 copy-start.27
  106.0 3.4 copy-start.41
  106.0 40.7 %copy-start.39 = (bf16[2,24]{1,0:T(2,128)(2,1)S(1)}, bf16[2,24]{1,0:T(2,128)(2,1)}, u32[]{:S(2)}) copy-start(bf16[2,24]{1,0:T(2,128)(2,1)} %param.22) | copy-start | bytes 292
  106.0 109.9 %copy-start.38 = (bf16[6,24]{1,0:T(8,128)(2,1)S(1)}, bf16[6,24]{1,0:T(8,128)(2,1)}, u32[]{:S(2)}) copy-start(bf16[6,24]{1,0:T(8,128)(2,1)} %param.20) | copy-start | bytes 868
  212.6 3.3 copy-start.25
  286.3 5.7 copy-start.16
  301.8 6.3 copy-start.24
  338.3 1.6 copy-start
  374.9 5.6 copy-start.1
  374.9 5.6 copy-start.35
  381.3 1.9 copy-start.2
  381.3 1.9 copy-start.26
  383.2 1.6 copy-start.34
  387.9 1.7 copy-start.3
  387.9 2.5 copy-start.22
  389.8 16.4 %copy-start.20 = (bf16[1024,768]{0,1:T(8,128)(2,1)}, bf16[1024,768]{0,1:T(8,128)(2,1)S(1)}, u32[]{:S(2)}) copy-start(bf16[1024,768]{0,1:T(8,128)(2,1)S(1)} %convert_element_type.126) | copy-start | bytes 4718596
  390.5 15.7 %copy-start.23 = (bf16[768,768]{1,0:T(8,128)(2,1)S(1)}, bf16[768,768]{1,0:T(8,128)(2,1)}, u32[]{:S(2)}) copy-start(bf16[768,768]{1,0:T(8,128)(2,1)} %all-gather.8.cloned.1.call-done) | copy-start | bytes 3538948
  406.2 5.1 copy-start.4
  413.6 3.4 copy-start.40
  415.3 1.7 copy-start.10
  433.5 1.9 copy-start.6
  435.4 4.0 copy-start.5
  446.2 7.1 copy-start.17
  453.3 2.0 copy-start.7
  458.0 1.9 copy-start.6
  459.9 4.0 copy-start.5
  470.7 7.1 copy-start.17
  477.8 2.0 copy-start.7
  486.6 8.1 copy-start.9
  501.3 1.9 copy-start.19
  504.4 3.2 copy-start.14
  504.4 3.3 copy-start.21
  507.6 203.5 %reduce-scatter.15.cloned.1.call-start = ((), (), s32[]{:S(2)}) async-start(), calls=%async_computation.9 | async-start | bytes 3244032
  514.4 300.3 %reduce-scatter.13.cloned.1.call-start = ((), (), s32[]{:S(2)}) async-start(), calls=%async_computation.8 | async-start | bytes 2433024 | tf_op jit(solution)/shard_map/reduce_scatter | solution.py:89
  521.6 5.3 copy-start.30
  521.6 5.4 copy-start.36
  521.6 5.4 copy-start.31
  521.6 397.9 %reduce-scatter.11.cloned.1.call-start = ((), (), s32[]{:S(2)}) async-start(), calls=%async_computation.7 | async-start | bytes 2433024 | tf_op jit(solution)/shard_map/reduce_scatter | solution.py:242
  526.9 3.0 copy-start.37
  526.9 3.0 copy-start.29
  526.9 3.0 copy-start.28
  526.9 3.1 copy-start.32
  527.0 5.1 copy-start.12
  532.1 3.9 copy-start.11
  (7 other events, 9.1 us)
Sparse Core Ops, SparseCore 0:
  10.9 57.2 all-gather.5
  71.1 53.4 all-gather.7
  127.5 53.8 all-gather.9
  507.8 96.8 reduce-scatter.16
  610.5 100.5 reduce-scatter.14
  716.8 97.9 reduce-scatter.12
  821.5 98.0 reduce-scatter.10
where the time goes:
time: 933 us; the launch traced here: 927 us
  waiting for transfers between devices  341 us (37%)
  blocking collectives  288 us (31%)
  matrix products  141 us (15%)
  local copies, waits for them, and re-layouts  95.8 us (10%)
  other arithmetic  44.8 us (5%)
  between operations  15.1 us (2%)
    unnamed x9, waiting for transfers between devices  133 us
    reduce_scatter x1, waiting for transfers between devices, local(): lax.psum_scatter(out_grad, ('dp', 'fsdp'), scatter_dimension=0, tiled=True)  105 us
    reduce_scatter x1, waiting for transfers between devices, reduce_ffn(): lax.psum_scatter(up_grad, ('dp', 'fsdp'), scatter_dimension=0, tiled=True)  104 us
    all_gather x1, blocking collectives, fetch_attention(): lax.all_gather(qkv_weight, ('dp', 'fsdp'), axis=0, tiled=True)  81.7 us
    unnamed x2, blocking collectives  76.7 us
    all_gather x1, blocking collectives, fetch_attention(): lax.all_gather(gains, ('dp', 'fsdp'), axis=1, tiled=True)  65.6 us
    all_gather x1, blocking collectives, fetch_attention(): lax.all_gather(biases, ('dp', 'fsdp'), axis=1, tiled=True)  63.9 us
    dot_general x3, matrix products, group_apply(): jnp.einsum('ngc,gce->nge', parts, table, preferred_element_type=jnp.float32)  42 us
  transfers between devices with their start and end apart: 7, of which 4 were waited for; matrix products, arithmetic and copies ran while one was open for 16% of the time, Pallas kernels for 0%

commit v1 on v0

--- a/solution.py
+++ b/solution.py
@@ -3,12 +3,27 @@
 import jax.numpy as jnp
 from jax import lax
 from jax.sharding import PartitionSpec as P
+from jax.lax import axis_index, axis_size, ppermute
 
 HEADS = 12
 GROUPS = 4
 EPSILON = 1e-05
 SCORE_SCALE = 0.125
 NEG_FILL = -1e30
+
+
+def number_the_classes(piece_in):
+    ax_name = ("dp", "fsdp")
+    step_out = axis_size(ax_name)
+    after = axis_index(ax_name)
+    ready, clean, newest = (step_out, after, piece_in.shape[0])
+    extra, found_now = (piece_in, 1)
+    while found_now < ready:
+        near = tuple(((i, (i - found_now) % ready) for i in range(ready)))
+        answer = ppermute(extra, axis_name=ax_name, perm=near)
+        extra = jnp.concatenate([extra, answer], axis=0)
+        found_now = 2 * found_now
+    return jnp.roll(extra, clean * newest, axis=0)
 
 
 def group_apply(values, weight):
@@ -107,7 +122,7 @@
 
     def fetch_attention():
         return (
-            lax.all_gather(qkv_weight, ("dp", "fsdp"), axis=0, tiled=True),
+            number_the_classes(qkv_weight),
             lax.all_gather(out_weight, ("dp", "fsdp"), axis=0, tiled=True),
             lax.all_gather(biases, ("dp", "fsdp"), axis=1, tiled=True),
             lax.all_gather(gains, ("dp", "fsdp"), axis=1, tiled=True),

time: 933 us -> 870 us (0.932)
  blocking collectives: 288 us -> 209 us
    all_gather x1 -> x0, blocking collectives: 81.7 us -> none  [fetch_attention(): lax.all_gather(qkv_weight, ('dp', 'fsdp'), axis=0, tiled=True)]
    unnamed x84 -> x92, local copies, waits for them, and re-layouts: 25.5 us -> 28.3 us
  transfers between devices with their start and end apart: 7 -> 12, of which waited for: 4 -> 6; matrix products, arithmetic and copies ran while one was open for 16% -> 17% of each run, Pallas kernels for 0% -> 0%
where the time goes in v1:
time: 870 us; the launch traced here: 866 us
  waiting for transfers between devices  348 us (40%)
  blocking collectives  209 us (24%)
  matrix products  140 us (16%)
  local copies, waits for them, and re-layouts  96.1 us (11%)
  other arithmetic  49.4 us (6%)
  between operations  15 us (2%)
    unnamed x9, waiting for transfers between devices  132 us
    reduce_scatter x1, waiting for transfers between devices, local(): lax.psum_scatter(out_grad, ('dp', 'fsdp'), scatter_dimension=0, tiled=True)  105 us
    reduce_scatter x1, waiting for transfers between devices, reduce_ffn(): lax.psum_scatter(up_grad, ('dp', 'fsdp'), scatter_dimension=0, tiled=True)  104 us
    unnamed x2, blocking collectives  79 us
    all_gather x1, blocking collectives, fetch_attention(): lax.all_gather(biases, ('dp', 'fsdp'), axis=1, tiled=True)  66.2 us
    all_gather x1, blocking collectives, fetch_attention(): lax.all_gather(gains, ('dp', 'fsdp'), axis=1, tiled=True)  63.7 us
    dot_general x3, matrix products, group_apply(): jnp.einsum('ngc,gce->nge', parts, table, preferred_element_type=jnp.float32)  40.3 us
    unnamed x92, local copies, waits for them, and re-layouts  28.3 us
  transfers between devices with their start and end apart: 12, of which 6 were waited for; matrix products, arithmetic and copies ran while one was open for 17% of the time, Pallas kernels for 0%

profile of v1, /device:TPU:0, one launch (start us, length us, event | category | flops | bytes accessed | tf_op | source)
XLA Modules:
  0.0 866.0 jit_solution(471273390161614439)
XLA Ops:
  8.7 6.4 collective-permute-start
  15.2 63.7 %all-gather.1 = bf16[32,24,2]{1,2,0:T(2,128)(2,1)S(1)} all-gather(bf16[1,24,2]{1,2,0:T(2,128)(2,1)} %bitcast.304), channel_id=1, replica_groups=mesh['dp'=4,'fsdp'=8] {'dp','fsdp'}, dimensions={0}, use_global_device_ids=true | all-gather | bytes 3168 | tf_op jit(solution)/shard_map/all_gather | solution.py:128
  79.8 2.7 convert_reduce_fusion.3
  85.6 40.2 %all-reduce = bf16[3072]{0:T(1024)(128)(2,1)S(1)} all-reduce(bf16[3072]{0:T(1024)(128)(2,1)S(1)} %dynamic-update-slice), channel_id=1, replica_groups=mesh['dp'=4,'fsdp'=8] {'dp','fsdp'}, use_global_device_ids=true, to_apply=%add | all-reduce | flops 3072 | bytes 12288
  126.9 66.2 %all-gather = bf16[32,24,6]{1,2,0:T(8,128)(2,1)S(1)} all-gather(bf16[1,24,6]{1,2,0:T(8,128)(2,1)} %bitcast.303), channel_id=1, replica_groups=mesh['dp'=4,'fsdp'=8] {'dp','fsdp'}, dimensions={0}, use_global_device_ids=true | all-gather | bytes 9504 | tf_op jit(solution)/shard_map/all_gather | solution.py:127
  195.0 5.1 collective-permute-done.2
  207.9 3.8 copy.94
  229.4 3.8 reshape.348
  233.2 2.9 convert_element_type.116
  236.4 5.7 reshape.347
  242.1 5.0 fusion.66
  248.4 21.1 %while.26 = (s32[]{:T(128)}, bf16[2,512,12,64]{1,3,2,0:T(8,128)(2,1)}, f32[2,12,512]{2,1,0:T(8,128)S(1)}, bf16[2,512,12,64]{1,3,2,0:T(8,128)(2,1)}, s32[2,512]{1...) while((s32[]{:T(128)}, ...), condition=%wide.region_3.5_spmd, body=%wide.region_0.4_spmd.sunk | while | flops 843836416 | bytes 42963044 | solution.py:161
  253.6 5.5 bitcast_dynamic-update-slice_fusion.10
  264.0 5.5 bitcast_dynamic-update-slice_fusion.10
  269.5 3.0 copy.100
  274.1 4.3 fusion.79
  281.8 33.3 %fusion.52 = (bf16[1024,4,768]{2,0,1:T(8,128)(2,1)}, f32[1024,4,768]{2,0,1:T(8,128)}, f32[4,1024,768]{2,1,0:T(8,128)}) fusion(f32[4,768]{1,0:T(4,128)S(1)} %copy-done.41, bf16[1024,4,192]{0,2,1:T(8,128)(2,1)} %bitcast.281, bf16[4,192,768]{2,1,0:T(8,128)(2,1)} %bitcast.294), kind=kOutput, calls=%fused_computation.77 | convolution fusion | flops 1415577600 | bytes 34222080 | tf_op jit(solution)/shard_map/ngc,gce->nge/dot_general | solution.py:32
  315.1 5.6 fusion.80
  325.0 3.2 fusion.73
  330.7 15.7 %convert_reduce_fusion = (f32[4,768]{1,0:T(4,128)}, bf16[1024,4,768]{2,0,1:T(8,128)(2,1)}) fusion(f32[1024,4,768]{2,0,1:T(8,128)} %get-tuple-element.276, bf16[1024,4,192]{0,2,1:T(8,128)(2,1)S(1)} %bitcast.285, bf16[4,768,192]{2,1,0:T(8,128)(2,1)S(1)} %bitcast.293, f32[4,1024,768]{2,1,0:T(8,128)} %get-tuple-element.296, f32[4,768]{1,0:T(4,128)S(1)} %copy-done.41), kind=kOutput, calls=%fused_computation.78 | convolution fusion | flops 1261433856 | bytes 34234368 | tf_op jit(solution)/shard_map/ipo,pso->ips/dot_general | solution.py:191
  346.4 5.1 fusion.81
  357.2 2.6 convolution_convert_fusion
  359.8 2.6 copy.107
  362.4 3.9 reshape.356
  366.2 2.9 copy.109
  373.2 49.2 %while.27 = (s32[]{:T(128)}, bf16[2,512,12,64]{1,3,2,0:T(8,128)(2,1)}, bf16[2,512,12,64]{1,3,2,0:T(8,128)(2,1)}, bf16[2,512,12,64]{1,3,2,0:T(8,128)(2,1)}, bf16[...) while((s32[]{:T(128)}, ...), condition=%wide.region_14.16_spmd, body=%wide.region_12.15_spmd.sunk | while | flops 2062019584 | bytes 143596848 | solution.py:218
  375.6 3.9 bitcast_dynamic-update-slice_fusion.14
  379.5 6.9 multiply_reduce_fusion.10
  386.4 7.1 multiply_convert_fusion.2
  400.1 3.9 bitcast_dynamic-update-slice_fusion.14
  404.0 6.9 multiply_reduce_fusion.10
  410.9 7.1 multiply_convert_fusion.2
  422.3 3.0 copy.111
  426.8 4.3 copy.112
  431.1 3.8 convert_element_type.135
  434.9 2.8 copy.110
  437.7 3.8 convert_element_type.131
  444.6 3.2 fusion.83
  447.9 6.7 fusion.85
  456.0 5.7 fusion.84
  461.9 5.2 fusion.70
  467.2 2.9 copy.124
  472.3 3.9 fusion.82
  479.4 38.9 %all-reduce.5 = (f32[6,768]{1,0:T(8,128)S(1)}, f32[3072]{0:T(1024)S(1)}, f32[2,768]{1,0:T(2,128)S(1)}) all-reduce(f32[6,768]{1,0:T(8,128)S(1)} %stack.36, f32[3072]{0:T(1024)S(1)} %reduce_sum.188, f32[2,768]{1,0:T(2,128)S(1)} %pad_maximum_fusion.3), channel_id=6, replica_groups=mesh['dp'=4,'fsdp'=8] {'dp','fsdp'}, use_global_device_ids=true, to_apply=%region_25.27.clone | all-reduce | flops 9216 | bytes 73728
  520.2 23.7 %reduce-scatter.17.cloned.1.call-done = f32[24,576]{1,0:T(8,128)} async-done(((f32[768,576]{1,0:T(8,128)}), f32[24,576]{1,0:T(8,128)}) %reduce-scatter.17.cloned.1.call-update) | async-done | bytes 55312
  543.9 106.5 %reduce-scatter.15.cloned.1.call-done = f32[96,192]{1,0:T(8,128)} async-done(((f32[3072,192]{1,0:T(8,128)}), f32[96,192]{1,0:T(8,128)}) %reduce-scatter.15.cloned.1.call-update) | async-done | bytes 73744
  650.4 103.7 %reduce-scatter.13.cloned.1.call-done = f32[24,768]{1,0:T(8,128)} async-done(((f32[768,768]{1,0:T(8,128)}), f32[24,768]{1,0:T(8,128)}) %reduce-scatter.13.cloned.1.call-update) | async-done | bytes 73744 | tf_op jit(solution)/shard_map/reduce_scatter | solution.py:104
  754.1 104.7 %reduce-scatter.11.cloned.1.call-done = f32[24,768]{1,0:T(8,128)} async-done(((f32[768,768]{1,0:T(8,128)}), f32[24,768]{1,0:T(8,128)}) %reduce-scatter.11.cloned.1.call-update) | async-done | bytes 73744 | tf_op jit(solution)/shard_map/reduce_scatter | solution.py:257
  (227 shorter events, 92.9 us)
Async XLA Ops:
  7.2 267.0 %all-gather.6.cloned.1.call-start = ((), (), s32[]{:S(2)}) async-start(), calls=%async_computation.4 | async-start | bytes 1216512 | tf_op jit(solution)/shard_map/all_gather | solution.py:126
  7.9 273.9 %all-gather.8.cloned.1.call-start = ((), (), s32[]{:S(2)}) async-start(), calls=%async_computation.5 | async-start | bytes 1216512 | tf_op jit(solution)/shard_map/all_gather | solution.py:133
  8.7 306.4 %all-gather.10.cloned.1.call-start = ((), (), s32[]{:S(2)}) async-start(), calls=%async_computation.6 | async-start | bytes 1622016 | tf_op jit(solution)/shard_map/all_gather | solution.py:134
  8.7 73.8 %collective-permute-start = (bf16[24,576]{1,0:T(8,128)(2,1)}, bf16[24,576]{1,0:T(8,128)(2,1)S(1)}, u32[]{:S(2)}, u32[]{:S(2)}) collective-permute-start(bf16[24,576]{1,0:T(8,128)(2,1)} %param.18), channel_id=1, source_target_pairs={{0,31},{1,0},{2,1},{3,2},{4,3},{5,4},{6,5},{7,6},{8,7},{9,8},{10,9... | collective-permute-start | bytes 82952 | tf_op jit(solution)/shard_map/ppermute | solution.py:23
  15.2 528.8 %reduce-scatter.17.cloned.1.call-start = ((), (), s32[]{:S(2)}) async-start(), calls=%async_computation.10 | async-start | bytes 2027520
  79.8 3.5 copy-start.29
  83.3 110.2 %collective-permute-start.1 = (bf16[48,576]{1,0:T(8,128)(2,1)S(1)}, bf16[48,576]{1,0:T(8,128)(2,1)S(1)}, u32[]{:S(2)}, u32[]{:S(2)}) collective-permute-start(bf16[48,576]{1,0:T(8,128)(2,1)S(1)} %pad_maximum_fusion.2), channel_id=1, source_target_pairs={{0,30},{1,31},{2,0},{3,1},{4,2},{5,3},{6,4},{7,5},{8,6},{9,7},{10,... | collective-permute-start | bytes 165896 | tf_op jit(solution)/shard_map/ppermute | solution.py:23
  194.3 5.8 collective-permute-start.2
  200.9 3.9 collective-permute-start.3
  205.6 2.2 copy-start.26
  205.6 14.6 %collective-permute-start.4 = (bf16[384,576]{1,0:T(8,128)(2,1)}, bf16[384,576]{1,0:T(8,128)(2,1)}, u32[]{:S(2)}, u32[]{:S(2)}) collective-permute-start(bf16[384,576]{1,0:T(8,128)(2,1)} %get-tuple-element.284), channel_id=1, source_target_pairs={{0,16},{1,17},{2,18},{3,19},{4,20},{5,21},{6,22},{7,23},{8,24},{9,... | collective-permute-start | bytes 1327112 | tf_op jit(solution)/shard_map/ppermute | solution.py:23
  207.9 6.1 copy-start.21
  220.2 4.2 copy-start.14
  242.1 6.3 copy-start.28
  278.9 2.9 copy-start.41
  315.1 5.6 copy-start.1
  315.1 5.6 copy-start.39
  321.5 1.9 copy-start.2
  321.5 1.9 copy-start.30
  328.1 2.5 copy-start.24
  330.0 16.4 %copy-start.22 = (bf16[1024,768]{0,1:T(8,128)(2,1)}, bf16[1024,768]{0,1:T(8,128)(2,1)S(1)}, u32[]{:S(2)}) copy-start(bf16[1024,768]{0,1:T(8,128)(2,1)S(1)} %convert_element_type.126) | copy-start | bytes 4718596
  330.7 15.7 %copy-start.25 = (bf16[768,768]{1,0:T(8,128)(2,1)S(1)}, bf16[768,768]{1,0:T(8,128)(2,1)}, u32[]{:S(2)}) copy-start(bf16[768,768]{1,0:T(8,128)(2,1)} %all-gather.8.cloned.1.call-done) | copy-start | bytes 3538948
  346.4 5.1 copy-start.4
  353.8 3.4 copy-start.43
  373.7 1.9 copy-start.6
  375.6 3.9 copy-start.5
  386.4 7.1 copy-start.18
  393.5 2.0 copy-start.7
  398.2 1.9 copy-start.6
  400.1 4.0 copy-start.5
  410.9 7.1 copy-start.18
  418.0 2.0 copy-start.7
  426.8 8.1 copy-start.9
  441.5 1.9 copy-start.20
  444.6 3.2 copy-start.16
  444.6 3.3 copy-start.23
  447.9 202.6 %reduce-scatter.15.cloned.1.call-start = ((), (), s32[]{:S(2)}) async-start(), calls=%async_computation.9 | async-start | bytes 3244032
  454.6 299.5 %reduce-scatter.13.cloned.1.call-start = ((), (), s32[]{:S(2)}) async-start(), calls=%async_computation.8 | async-start | bytes 2433024 | tf_op jit(solution)/shard_map/reduce_scatter | solution.py:104
  461.8 5.4 copy-start.34
  461.8 5.4 copy-start.40
  461.8 5.4 copy-start.35
  461.8 397.0 %reduce-scatter.11.cloned.1.call-start = ((), (), s32[]{:S(2)}) async-start(), calls=%async_computation.7 | async-start | bytes 2433024 | tf_op jit(solution)/shard_map/reduce_scatter | solution.py:257
  467.1 3.0 copy-start.42
  467.1 3.0 copy-start.33
  467.1 3.1 copy-start.32
  467.1 3.1 copy-start.36
  467.2 5.1 copy-start.13
  472.3 4.0 copy-start.11
  (14 other events, 20.4 us)
Sparse Core Ops, SparseCore 0:
  10.9 56.8 all-gather.5
  70.7 53.1 all-gather.7
  126.9 54.0 all-gather.9
  448.0 95.8 reduce-scatter.16
  549.8 100.5 reduce-scatter.14
  656.1 97.9 reduce-scatter.12
  760.8 97.9 reduce-scatter.10
